TPU v7x, 512 devices: a whole 4x4x16 slice. The times are simulated.
512 devices in a mesh: cells: 64 (over z, x), snaps: 8 (over y, core).
Axes of the slice: x: 4, y: 4, z: 16, core: 2. Of those that a mesh axis runs over, the one named last changes fastest.
Arguments:
- snapshots: float32 [262144, 2048], P('cells', 'snaps'), may hold values from -6 to 6
- sketch: float32 [2048, 32], P('snaps'), may hold values from -6 to 6
Outputs:
- basis: float32 [32, 262144], P(None, 'cells')
- coefficients: float32 [32, 2048], P(None, 'snaps')
All inputs are finite; a program needn't handle non-finite values.
Results may differ from a plain program's by a relative error of at most 0.0003.
Values sent between devices are 32-bit elements; how exact they have to be, the bound alone decides.
A program may use at most 64 MiB of HBM per device.

v0:
```python
import math
import jax
import jax.numpy as jnp
from jax import lax
from jax.sharding import PartitionSpec as P


def partner_2(block, axis, distance):
    count = lax.axis_size(axis)
    route = []
    for low in range(count):
        high = low | 1 << distance
        if high != low and high < count:
            route += [(low, high), (high, low)]
    return lax.ppermute(block, axis, route)


def upper_factor(columns):
    count = columns.shape[0]
    places = jnp.arange(columns.shape[1])
    for step in range(count):
        column = columns[step]
        lower_part = jnp.where(places >= step, column, 0.0)
        length = jnp.sqrt(jnp.sum(lower_part * lower_part))
        sense = jnp.where(column[step] < 0, -1.0, 1.0)
        vector = lower_part + jnp.where(places == step, sense * length, 0.0)
        factor = 2.0 / jnp.sum(vector * vector)
        inner = jnp.dot(columns, vector, precision=lax.Precision.HIGHEST)
        columns = columns - factor * inner[:, None] * vector[None, :]
    upper = jnp.triu(columns[:, :count].T)
    diagonal = jnp.diagonal(upper)
    return jnp.where(diagonal[:, None] < 0, -upper, upper)


def lower_solve(lower_factor, rows):
    return lax.linalg.triangular_solve(lower_factor, rows, left_side=True, lower=True)


def upper_solve(upper, rows):
    return lower_solve(jnp.transpose(upper), rows)


def shards(snapshots, sketch):
    partial_rows = jnp.einsum("sk,ms->km", sketch, snapshots, precision=lax.Precision.HIGHEST)
    sketched = lax.psum(partial_rows, "snaps")
    total_cells = snapshots.shape[0] * lax.axis_size("cells")
    upper = upper_factor(sketched)
    position = lax.axis_index("cells")
    for bit in range(lax.axis_size("cells").bit_length() - 1):
        partner = partner_2(upper, "cells", bit)
        high_side = jnp.right_shift(position, bit) % 2 == 1
        first = jnp.where(high_side, partner, upper)
        second = jnp.where(high_side, upper, partner)
        upper = upper_factor(jnp.concatenate([first.T, second.T], axis=1))
    orth = upper_solve(upper, sketched)
    partial_coeffs = jnp.dot(orth, snapshots, precision=lax.Precision.HIGHEST)
    coefficients = lax.psum(partial_coeffs, "cells")
    basis = orth * math.sqrt(total_cells)
    return (basis, coefficients)


def solution(mesh):
    return jax.shard_map(
        shards,
        mesh=mesh,
        in_specs=(P("cells", "snaps"), P("snaps", None)),
        out_specs=(P(None, "cells"), P(None, "snaps")),
        check_vma=False,
    )
```

profile of v0, /device:TPU:8, one launch (start us, length us, event | category | flops | bytes accessed | tf_op | source)
XLA Modules:
  0.0 1405.5 jit_solution(5781502194587796289)
XLA Ops:
  7.9 6.8 fusion.519
  14.8 78.8 %all-reduce.2.cloned.1.call-done = f32[32,4096]{1,0:T(8,128)} async-done(((f32[32,4096]{1,0:T(8,128)}), f32[32,4096]{1,0:T(8,128)}) %all-reduce.2.cloned.1.call-update) | async-done | bytes 524304 | tf_op jit(solution)/shard_map/psum | solution.py:45
  99.9 1.6 fusion.223
  235.0 1.3 multiply_subtract_fusion.4
  240.7 1.4 multiply_subtract_fusion.3
  246.5 1.6 multiply_subtract_fusion.2
  252.5 1.5 multiply_subtract_fusion.1
  258.4 1.6 multiply_subtract_fusion
  265.3 3.4 collective-permute-start
  268.6 2.2 collective-permute-done
  403.5 5.3 collective-permute-start.1
  408.8 1.8 collective-permute-done.1
  543.2 3.6 collective-permute-start.2
  546.8 2.0 collective-permute-done.2
  681.4 4.7 collective-permute-start.3
  686.1 1.8 collective-permute-done.3
  820.5 7.9 collective-permute-start.4
  828.4 1.6 collective-permute-done.4
  962.7 13.1 collective-permute-start.5
  975.8 1.5 collective-permute-done.5
  1109.9 2.4 custom-call.3
  1112.4 1.4 broadcast_multiply_fusion
  1113.8 4.3 fusion.520
  1118.1 280.0 %psum.15 = f32[32,256]{1,0:T(8,128)} all-reduce(f32[32,256]{1,0:T(8,128)S(1)} %fusion.520), channel_id=1, replica_groups=mesh['cells'=64,'snaps'=8] {'cells'}, use_global_device_ids=true, to_apply=%region_449.450 | all-reduce | flops 8192 | bytes 65536 | tf_op jit(solution)/shard_map/psum | solution.py:57
  (1406 shorter events, 500.9 us)
Async XLA Ops:
  7.2 0.8 copy-start
  7.2 86.4 %all-reduce.2.cloned.1.call-start = ((), (), s32[]{:S(2)}) async-start(), calls=%async_computation | async-start | bytes 1048576 | tf_op jit(solution)/shard_map/psum | solution.py:45
  93.6 19.1 %copy-start.1 = (f32[32,4096]{1,0:T(8,128)S(1)}, f32[32,4096]{1,0:T(8,128)}, u32[]{:S(2)}) copy-start(f32[32,4096]{1,0:T(8,128)} %all-reduce.2.cloned.1.call-done) | copy-start | bytes 1572868
  265.3 5.6 collective-permute-start
  403.5 7.1 collective-permute-start.1
  543.2 5.6 collective-permute-start.2
  681.4 6.5 collective-permute-start.3
  820.5 9.5 collective-permute-start.4
  962.7 14.6 %collective-permute-start.5 = (f32[32,32]{0,1:T(8,128)S(1)}, f32[32,32]{0,1:T(8,128)S(1)}, u32[]{:S(2)}, u32[]{:S(2)}) collective-permute-start(f32[32,32]{0,1:T(8,128)S(1)} %negate_select_fusion.1), channel_id=1, source_target_pairs={{0,256},{256,0},{8,264},{264,8},{16,272},{272,16},{24,280},{280,24... | collective-permute-start | bytes 12296 | tf_op jit(solution)/shard_map/ppermute | solution.py:15
Sparse Core Ops, SparseCore 0:
  14.9 78.6 all-reduce.1
where the time goes:
time: 1420 us; the launch traced here: 1410 us
  between operations  473 us (33%)
  other arithmetic  330 us (23%)
  blocking collectives  280 us (20%)
  local copies, waits for them, and re-layouts  138 us (10%)
  waiting for transfers between devices  89.8 us (6%)
  matrix products  56.3 us (4%)
  starting transfers between devices  38 us (3%)
    psum x1, blocking collectives, shards(): coefficients = lax.psum(partial_coeffs, 'cells')  280 us
    reduce_sum x224, other arithmetic, upper_factor(): factor = 2.0 / jnp.sum(vector * vector)  135 us
    reduce_sum x224, other arithmetic, upper_factor(): length = jnp.sqrt(jnp.sum(lower_part * lower_part))  135 us
    slice x224, local copies, waits for them, and re-layouts, upper_factor(): sense = jnp.where(column[step] < 0, -1.0, 1.0)  131 us
    psum x1, waiting for transfers between devices, shards(): sketched = lax.psum(partial_rows, 'snaps')  78.8 us
    sub x217, other arithmetic, upper_factor(): columns = columns - factor * inner[:, None] * vector[None, :]  53.5 us
    dot_general x224, matrix products, upper_factor(): inner = jnp.dot(columns, vector, precision=lax.Precision.HIGHEST)  43.8 us
    ppermute x6, starting transfers between devices, partner_2(): return lax.ppermute(block, axis, route)  37.9 us
  transfers between devices with their start and end apart: 7, of which 7 were waited for; matrix products, arithmetic and copies ran while one was open for 0% of the time, Pallas kernels for 0%

commit v1 on v0

--- a/solution.py
+++ b/solution.py
@@ -42,7 +42,11 @@
 
 def shards(snapshots, sketch):
     partial_rows = jnp.einsum("sk,ms->km", sketch, snapshots, precision=lax.Precision.HIGHEST)
-    sketched = lax.psum(partial_rows, "snaps")
+    sketched = partial_rows
+    for hop in (1, 2, 4):
+        sketched = sketched + lax.ppermute(
+            sketched, "snaps", [(dev, dev ^ hop) for dev in range(8)]
+        )
     total_cells = snapshots.shape[0] * lax.axis_size("cells")
     upper = upper_factor(sketched)
     position = lax.axis_index("cells")

time: 1420 us -> 1360 us (0.958)
  the two profiles are of different devices: /device:TPU:8 before, /device:TPU:16 now
where the time goes in v1:
time: 1360 us; the launch traced here: 1350 us
  between operations  459 us (34%)
  other arithmetic  328 us (24%)
  blocking collectives  283 us (21%)
  local copies, waits for them, and re-layouts  137 us (10%)
  matrix products  54.1 us (4%)
  waiting for transfers between devices  44.4 us (3%)
  starting transfers between devices  43.5 us (3%)
    psum x1, blocking collectives, shards(): coefficients = lax.psum(partial_coeffs, 'cells')  283 us
    reduce_sum x224, other arithmetic, upper_factor(): factor = 2.0 / jnp.sum(vector * vector)  135 us
    reduce_sum x224, other arithmetic, upper_factor(): length = jnp.sqrt(jnp.sum(lower_part * lower_part))  135 us
    slice x224, local copies, waits for them, and re-layouts, upper_factor(): sense = jnp.where(column[step] < 0, -1.0, 1.0)  130 us
    sub x217, other arithmetic, upper_factor(): columns = columns - factor * inner[:, None] * vector[None, :]  51.9 us
    dot_general x224, matrix products, upper_factor(): inner = jnp.dot(columns, vector, precision=lax.Precision.HIGHEST)  42.4 us
    ppermute x6, starting transfers between devices, partner_2(): return lax.ppermute(block, axis, route)  30.6 us
  transfers between devices with their start and end apart: 9, of which 9 were waited for; matrix products, arithmetic and copies ran while one was open for 0% of the time, Pallas kernels for 0%

profile of v1, /device:TPU:16, one launch (start us, length us, event | category | flops | bytes accessed | tf_op | source)
XLA Modules:
  0.0 1348.2 jit_solution(16442868913173157111)
XLA Ops:
  1.4 6.0 fusion.519
  7.4 1.9 collective-permute-start
  9.3 1.9 collective-permute-done
  11.3 3.2 collective-permute-start.1
  14.5 12.7 collective-permute-done.1
  27.2 7.8 collective-permute-start.2
  35.0 11.2 collective-permute-done.2
  164.9 1.5 multiply_subtract_fusion.7
  199.4 1.5 multiply_subtract_fusion.1
  205.2 1.8 multiply_subtract_fusion
  212.3 1.9 collective-permute-start.3
  214.2 3.7 collective-permute-done.3
  350.5 2.7 collective-permute-start.4
  353.2 4.4 collective-permute-done.4
  490.2 2.2 collective-permute-start.5
  492.4 3.4 collective-permute-done.5
  628.4 3.2 collective-permute-start.6
  631.7 3.3 collective-permute-done.6
  767.6 7.2 collective-permute-start.7
  774.8 2.3 collective-permute-done.7
  909.7 13.5 collective-permute-start.8
  1057.3 2.4 custom-call.3
  1061.2 4.3 fusion.520
  1065.5 282.5 %psum.7 = f32[32,256]{1,0:T(8,128)} all-reduce(f32[32,256]{1,0:T(8,128)S(1)} %fusion.520), channel_id=1, replica_groups=mesh['cells'=64,'snaps'=8] {'cells'}, use_global_device_ids=true, to_apply=%region_448.449 | all-reduce | flops 8192 | bytes 65536 | tf_op jit(solution)/shard_map/psum | solution.py:61
  (1410 shorter events, 502.5 us)
Async XLA Ops:
  0.6 0.8 copy-start
  7.4 3.8 collective-permute-start
  11.3 15.9 %collective-permute-start.1 = (f32[32,4096]{1,0:T(8,128)S(1)}, f32[32,4096]{1,0:T(8,128)S(1)}, u32[]{:S(2)}, u32[]{:S(2)}) collective-permute-start(f32[32,4096]{1,0:T(8,128)S(1)} %add.1435), channel_id=1, source_target_pairs={{0,2},{1,3},{2,0},{3,1},{4,6},{5,7},{6,4},{7,5},{8,10},{9,11},{10,... | collective-permute-start | bytes 1572872 | tf_op jit(solution)/shard_map/ppermute | solution.py:47
  27.2 19.0 %collective-permute-start.2 = (f32[32,4096]{1,0:T(8,128)S(1)}, f32[32,4096]{1,0:T(8,128)S(1)}, u32[]{:S(2)}, u32[]{:S(2)}) collective-permute-start(f32[32,4096]{1,0:T(8,128)S(1)} %add.1436), channel_id=1, source_target_pairs={{0,4},{1,5},{2,6},{3,7},{4,0},{5,1},{6,2},{7,3},{8,12},{9,13},{10,... | collective-permute-start | bytes 1572872 | tf_op jit(solution)/shard_map/ppermute | solution.py:47
  212.3 5.6 collective-permute-start.3
  350.5 7.1 collective-permute-start.4
  490.2 5.6 collective-permute-start.5
  628.4 6.5 collective-permute-start.6
  767.6 9.5 collective-permute-start.7
  909.7 15.0 %collective-permute-start.8 = (f32[32,32]{0,1:T(8,128)S(1)}, f32[32,32]{0,1:T(8,128)S(1)}, u32[]{:S(2)}, u32[]{:S(2)}) collective-permute-start(f32[32,32]{0,1:T(8,128)S(1)} %negate_select_fusion.1), channel_id=1, source_target_pairs={{0,256},{256,0},{8,264},{264,8},{16,272},{272,16},{24,280},{280,24... | collective-permute-start | bytes 12296 | tf_op jit(solution)/shard_map/ppermute | solution.py:15
